TPU v7x, 256 devices: a whole 4x4x8 slice. The times are simulated.
256 devices in a mesh: bx: 4 (over x), by: 32 (over y, z), gz: 2 (over core).
Axes of the slice: x: 4, y: 4, z: 8, core: 2. Of those that a mesh axis runs over, the one named last changes fastest.
Arguments:
- electric_start: float32 [3, 512, 64, 256], P(None, 'by', 'bx', 'gz'), may hold values from -6 to 6
- magnetic_start: float32 [3, 512, 64, 256], P(None, 'by', 'bx', 'gz'), may hold values from -6 to 6
- current_start: float32 [3, 512, 64, 256], P(None, 'by', 'bx', 'gz'), may hold values from -6 to 6
- cotangent: float32 [3, 512, 64, 256], P(None, 'by', 'bx', 'gz'), may hold values from -6 to 6
- level_set: float32 [512, 64, 256], P('by', 'bx', 'gz'), may hold values from -8 to 8
- material: int32 [512, 64, 256], P('by', 'bx', 'gz'), may hold values from 0 to 2
- source_cell: int32 [2048], P(('bx', 'by', 'gz')), may hold values from 0 to 32767
- basis: bfloat16 [65536, 64, 256], P(('bx', 'by', 'gz')), may hold values from 0 to 1
- block_owner: int32 [65536, 1], P(('bx', 'by', 'gz')), may hold values from 0 to 127; in each aligned block of 256 rows (0 to 255, 256 to 511, ...) at most 4 rows name the same one
- block_group: int32 [65536], P(('bx', 'by', 'gz')), may hold values from 0 to 127
Outputs:
- final_electric: float32 [3, 512, 64, 256], P(None, 'by', 'bx', 'gz')
- adjoint_electric: float32 [3, 512, 64, 256], P(None, 'by', 'bx', 'gz')
- coef_grad: float32 [64, 32768], P(None, ('bx', 'by', 'gz'))
Inputs may be any that keep to these rules, and one draw needn't show every extreme that they name: `material`: 0 is vacuum, 1 design dielectric, 2 silver. `source_cell`: a flat cell index within the device's own brick; a cell may be named more than once. `block_owner`: among the 256 blocks of one device no owner is named by more than 4 blocks, and in some device one owner is named by exactly 4.
All inputs are finite; a program needn't handle non-finite values.
Results may differ from a plain program's by a relative error of at most 0.0029.
Values sent between devices are 32-bit elements; how exact they have to be, the bound alone decides.
A program may use at most 64 MiB of HBM per device.

v0:
```python
import jax
import jax.numpy as jnp
from jax import lax
from jax.sharding import PartitionSpec as P

NSTEP = 2
KB = 64
GRP_DEV = 128
time_step = 0.5
drude_keep = 0.9
drude_gain = 1.0
metal_permit = 3.0
design_contrast = 5.0
source_level = 3.0
source_wave = (1.0, -0.6, 0.8, -0.4)


def passed_along(x, axis, by):
    count = lax.axis_size(axis)
    pairs = [(i, i + by) for i in range(count) if 0 <= i + by < count]
    return lax.ppermute(x, axis, pairs)


def face_y(face_cells, offset):
    return passed_along(face_cells, "by", offset)


def face_x(face_cells, offset):
    return passed_along(face_cells, "bx", offset)


def face_z(face_cells, offset):
    return passed_along(face_cells, "gz", offset)


def beside(couple, axis_dim, offset):
    length = couple.shape[axis_dim]
    border_at = 0 if offset < 0 else length - 1
    face_cells = lax.index_in_dim(couple, border_at, axis=axis_dim, keepdims=False)
    if axis_dim == 1:
        arrived = face_y(face_cells, offset)
    elif axis_dim == 2:
        arrived = face_x(face_cells, offset)
    else:
        flattened = face_cells.reshape(face_cells.shape[0], -1)
        arrived = face_z(flattened, offset).reshape(face_cells.shape)
    arrived = jnp.expand_dims(arrived, axis_dim)
    if offset < 0:
        return jnp.concatenate(
            [lax.slice_in_dim(couple, 1, length, axis=axis_dim), arrived], axis=axis_dim
        )
    return jnp.concatenate(
        [arrived, lax.slice_in_dim(couple, 0, length - 1, axis=axis_dim)], axis=axis_dim
    )


def differ(couple, axis_dim, offset):
    neighbour = beside(couple, axis_dim, offset)
    if offset < 0:
        return neighbour - couple
    return couple - neighbour


def curl(fields, offset):
    along_x = differ(jnp.stack([fields[1], fields[2]]), 2, offset)
    along_y = differ(jnp.stack([fields[0], fields[2]]), 1, offset)
    along_z = differ(jnp.stack([fields[0], fields[1]]), 3, offset)
    return jnp.stack([along_y[1] - along_z[1], along_z[0] - along_x[1], along_x[0] - along_y[0]])


def local(
    electric_start,
    magnetic_start,
    current_start,
    cotangent,
    level_set,
    material,
    source_cell,
    basis,
    block_owner,
    block_group,
):
    silver = (material == 2).astype(jnp.float32)
    design = (material == 1).astype(jnp.float32)
    smooth = jax.nn.sigmoid(level_set)
    permit = jnp.where(
        material == 2, metal_permit, jnp.where(material == 1, 1.0 + design_contrast * smooth, 1.0)
    )
    sources = (
        jnp.zeros((material.size,), jnp.float32).at[source_cell].add(1.0).reshape(material.shape)
    )
    electric, magnetic, current = (electric_start, magnetic_start, current_start)
    drives = []
    for moment in range(NSTEP):
        magnetic = magnetic - time_step * curl(electric, -1)
        current = silver * (drude_keep * current + drude_gain * electric)
        drive_term = curl(magnetic, 1) - current
        electric = electric + time_step / permit * drive_term
        electric = electric.at[2].add(source_level * source_wave[moment] * sources)
        drives.append(drive_term)
    step_ratio = time_step / permit
    adj_electric = cotangent
    adj_magnetic = jnp.zeros_like(cotangent)
    adj_current = jnp.zeros_like(cotangent)
    eps_grad = jnp.zeros(material.shape, jnp.float32)
    for moment in reversed(range(NSTEP)):
        scaled = step_ratio * adj_electric
        eps_grad = eps_grad - jnp.sum(scaled * drives[moment], axis=0) / permit
        adj_drive = adj_current - scaled
        adj_magnetic = adj_magnetic + curl(scaled, -1)
        adj_electric = (
            adj_electric + drude_gain * silver * adj_drive - time_step * curl(adj_magnetic, 1)
        )
        adj_current = drude_keep * silver * adj_drive
    level_grad = eps_grad * design * design_contrast * (smooth * (1.0 - smooth))
    cell_grad = level_grad.astype(jnp.bfloat16)
    tile_width = basis.shape[2]
    tile_count = cell_grad.size // tile_width
    block_count = basis.shape[0]
    tile_fan = block_count // tile_count
    cell_tiles = cell_grad.reshape(tile_count, tile_width)
    blocks = basis.reshape(tile_count, tile_fan, KB, tile_width)
    partials = jnp.einsum(
        "tfkc,tc->tfk", blocks, cell_tiles, preferred_element_type=jnp.float32
    ).reshape(block_count, KB)
    size_bx = lax.axis_size("bx")
    planes = size_bx * lax.axis_size("by")
    capacity = max(2, 2 * block_count // planes)
    slots = planes * capacity
    owner_plane = block_owner[:, 0]
    owner_hits = (owner_plane[:, None] == jnp.arange(planes, dtype=jnp.int32)[None, :]).astype(
        jnp.float32
    )
    before = jnp.cumsum(owner_hits, axis=0) - owner_hits
    slot_rank = jnp.sum(before * owner_hits, axis=1).astype(jnp.int32)
    target = owner_plane * capacity + slot_rank
    placing = (target[:, None] == jnp.arange(slots, dtype=jnp.int32)[None, :]).astype(jnp.float32)
    send_vals = jnp.einsum("bk,bs->ks", partials, placing, precision=lax.Precision.HIGHEST)
    send_ids = (
        jnp.einsum(
            "b,bs->s",
            block_group.astype(jnp.float32) + 1.0,
            placing,
            precision=lax.Precision.HIGHEST,
        )[None, :]
        - 1.0
    )
    got_vals, got_ids = (
        lax.all_to_all(send_vals, ("bx", "by"), split_axis=1, concat_axis=1, tiled=True),
        lax.all_to_all(send_ids, ("bx", "by"), split_axis=1, concat_axis=1, tiled=True),
    )
    group_hits = (
        got_ids[0][:, None] == jnp.arange(GRP_DEV, dtype=jnp.int32)[None, :].astype(jnp.float32)
    ).astype(jnp.float32)
    coef_grad = jnp.dot(got_vals, group_hits, precision=lax.Precision.HIGHEST)
    return (electric, adj_electric, coef_grad)


def solution(mesh):
    return jax.shard_map(
        local,
        mesh=mesh,
        in_specs=(
            P(None, "by", "bx", "gz"),
            P(None, "by", "bx", "gz"),
            P(None, "by", "bx", "gz"),
            P(None, "by", "bx", "gz"),
            P("by", "bx", "gz"),
            P("by", "bx", "gz"),
            P(("bx", "by", "gz")),
            P(("bx", "by", "gz"), None, None),
            P(("bx", "by", "gz"), None),
            P(("bx", "by", "gz")),
        ),
        out_specs=(
            P(None, "by", "bx", "gz"),
            P(None, "by", "bx", "gz"),
            P(None, ("bx", "by", "gz")),
        ),
        check_vma=False,
    )
```

profile of v0, /device:TPU:4, one launch (start us, length us, event | category | flops | bytes accessed | tf_op | source)
XLA Modules:
  0.0 176.0 jit_solution(5927105462938856978)
XLA Ops:
  6.5 2.4 %collective-permute-start.2 = (f32[2,16,128]{2,1,0:T(8,128)S(1)}, f32[2,16,128]{2,1,0:T(8,128)S(1)}, u32[]{:S(2)}, u32[]{:S(2)}) collective-permute-start(f32[2,16,128]{2,1,0:T(8,128)S(1)} %bitcast.135), channel_id=1, source_target_pairs={{64,0},{128,64},{192,128},{65,1},{129,65},{193,129},{66,2},{130,66... | collective-permute-start | bytes 49160 | tf_op jit(solution)/shard_map/ppermute | solution.py:21
  13.4 16.9 %all-to-all-start.1 = ((f32[1,128,4]{2,0,1:T(1,128)}), f32[1,128,4]{2,0,1:T(1,128)S(1)}, u32[]{:S(2)}, u32[]{:S(2)}) async-start(f32[1,128,4]{2,0,1:T(1,128)} %bitcast.57), calls=%async_computation.1 | async-start | bytes 131072 | tf_op jit(solution)/shard_map/all_to_all | solution.py:150
  34.6 1.6 fusion.42
  47.1 2.6 %collective-permute-start.3 = (f32[2,16,128]{2,1,0:T(8,128)}, f32[2,16,128]{2,1,0:T(8,128)S(1)}, u32[]{:S(2)}, u32[]{:S(2)}) collective-permute-start(f32[2,16,128]{2,1,0:T(8,128)} %fusion.58), channel_id=1, source_target_pairs={{0,2},{2,4},{4,6},{6,8},{8,10},{10,12},{12,14},{14,16},{16,18},{18... | collective-permute-start | bytes 49160 | tf_op jit(solution)/shard_map/ppermute | solution.py:21
  49.8 1.9 %collective-permute-start.4 = (f32[2,256]{1,0:T(2,128)S(1)}, f32[2,256]{1,0:T(2,128)}, u32[]{:S(2)}, u32[]{:S(2)}) collective-permute-start(f32[2,256]{1,0:T(2,128)S(1)} %reshape_squeeze.25), channel_id=1, source_target_pairs={{0,1},{2,3},{4,5},{6,7},{8,9},{10,11},{12,13},{14,15},{16,17},{18,... | collective-permute-start | bytes 6152 | tf_op jit(solution)/shard_map/ppermute | solution.py:21
  52.4 3.1 %collective-permute-start.5 = (f32[2,16,128]{2,1,0:T(8,128)}, f32[2,16,128]{2,1,0:T(8,128)S(1)}, u32[]{:S(2)}, u32[]{:S(2)}) collective-permute-start(f32[2,16,128]{2,1,0:T(8,128)} %bitcast.8), channel_id=1, source_target_pairs={{0,64},{64,128},{128,192},{1,65},{65,129},{129,193},{2,66},{66,130... | collective-permute-start | bytes 49160 | tf_op jit(solution)/shard_map/ppermute | solution.py:21
  56.5 1.7 collective-permute-done.5
  69.7 3.0 %collective-permute-start.8 = (f32[2,16,128]{2,1,0:T(8,128)S(1)}, f32[2,16,128]{2,1,0:T(8,128)S(1)}, u32[]{:S(2)}, u32[]{:S(2)}) collective-permute-start(f32[2,16,128]{2,1,0:T(8,128)S(1)} %bitcast.136), channel_id=1, source_target_pairs={{64,0},{128,64},{192,128},{65,1},{129,65},{193,129},{66,2},{130,66... | collective-permute-start | bytes 49160 | tf_op jit(solution)/shard_map/ppermute | solution.py:21
  74.0 1.9 %collective-permute-start.14 = (f32[2,16,128]{2,1,0:T(8,128)}, f32[2,16,128]{2,1,0:T(8,128)S(1)}, u32[]{:S(2)}, u32[]{:S(2)}) collective-permute-start(f32[2,16,128]{2,1,0:T(8,128)} %bitcast.25), channel_id=1, source_target_pairs={{64,0},{128,64},{192,128},{65,1},{129,65},{193,129},{66,2},{130,66... | collective-permute-start | bytes 49160 | tf_op jit(solution)/shard_map/ppermute | solution.py:21
  86.2 5.2 %collective-permute-start.9 = (f32[2,16,128]{2,1,0:T(8,128)S(1)}, f32[2,16,128]{2,1,0:T(8,128)S(1)}, u32[]{:S(2)}, u32[]{:S(2)}) collective-permute-start(f32[2,16,128]{2,1,0:T(8,128)S(1)} %fusion.60), channel_id=1, source_target_pairs={{0,2},{2,4},{4,6},{6,8},{8,10},{10,12},{12,14},{14,16},{16,18},{18... | collective-permute-start | bytes 49160 | tf_op jit(solution)/shard_map/ppermute | solution.py:21
  91.5 2.5 %collective-permute-start.10 = (f32[2,256]{1,0:T(2,128)S(1)}, f32[2,256]{1,0:T(2,128)S(1)}, u32[]{:S(2)}, u32[]{:S(2)}) collective-permute-start(f32[2,256]{1,0:T(2,128)S(1)} %reshape_squeeze.27), channel_id=1, source_target_pairs={{0,1},{2,3},{4,5},{6,7},{8,9},{10,11},{12,13},{14,15},{16,17},{18,... | collective-permute-start | bytes 6152 | tf_op jit(solution)/shard_map/ppermute | solution.py:21
  96.8 3.6 %collective-permute-start.11 = (f32[2,16,128]{2,1,0:T(8,128)S(1)}, f32[2,16,128]{2,1,0:T(8,128)S(1)}, u32[]{:S(2)}, u32[]{:S(2)}) collective-permute-start(f32[2,16,128]{2,1,0:T(8,128)S(1)} %bitcast.137), channel_id=1, source_target_pairs={{0,64},{64,128},{128,192},{1,65},{65,129},{129,193},{2,66},{66,130... | collective-permute-start | bytes 49160 | tf_op jit(solution)/shard_map/ppermute | solution.py:21
  100.4 1.9 %collective-permute-start.17 = (f32[2,16,128]{2,1,0:T(8,128)S(1)}, f32[2,16,128]{2,1,0:T(8,128)S(1)}, u32[]{:S(2)}, u32[]{:S(2)}) collective-permute-start(f32[2,16,128]{2,1,0:T(8,128)S(1)} %bitcast.129), channel_id=1, source_target_pairs={{0,64},{64,128},{128,192},{1,65},{65,129},{129,193},{2,66},{66,130... | collective-permute-start | bytes 49160 | tf_op jit(solution)/shard_map/ppermute | solution.py:21
  102.4 3.6 %collective-permute-start.15 = (f32[2,16,128]{2,1,0:T(8,128)S(1)}, f32[2,16,128]{2,1,0:T(8,128)S(1)}, u32[]{:S(2)}, u32[]{:S(2)}) collective-permute-start(f32[2,16,128]{2,1,0:T(8,128)S(1)} %fusion.56), channel_id=1, source_target_pairs={{0,2},{2,4},{4,6},{6,8},{8,10},{10,12},{12,14},{14,16},{16,18},{18... | collective-permute-start | bytes 49160 | tf_op jit(solution)/shard_map/ppermute | solution.py:21
  118.1 6.7 %fusion.70 = f32[128,1,2,64]{3,1,2,0:T(1,128)S(1)} fusion(bf16[128,256,1,1]{1,2,3,0:T(2,128)(2,1)S(1)} %reshape.178, bf16[128,2,64,256]{3,2,1,0:T(8,128)(2,1)} %bitcast.110), kind=kOutput, calls=%fused_computation.204 | convolution fusion | flops 8388608 | bytes 8519680 | tf_op jit(solution)/shard_map/tfkc,tc->tfk/dot_general | solution.py:123
  128.4 1.9 %reshape.198 = f32[128,1,256]{2,1,0:T(1,128)} reshape(f32[128,4,64]{2,1,0:T(4,128)} %bitcast.112) | data formatting | bytes 262144
  130.3 17.0 %all-to-all-start = ((f32[128,1,256]{2,1,0:T(1,128)}), f32[128,1,256]{2,1,0:T(1,128)}, u32[]{:S(2)}, u32[]{:S(2)}) async-start(f32[128,1,256]{2,1,0:T(1,128)} %reshape.198), calls=%async_computation | async-start | bytes 262144 | tf_op jit(solution)/shard_map/all_to_all | solution.py:149
  147.3 2.3 %collective-permute-start.20 = (f32[2,16,128]{2,1,0:T(8,128)}, f32[2,16,128]{2,1,0:T(8,128)S(1)}, u32[]{:S(2)}, u32[]{:S(2)}) collective-permute-start(f32[2,16,128]{2,1,0:T(8,128)} %bitcast.138), channel_id=1, source_target_pairs={{64,0},{128,64},{192,128},{65,1},{129,65},{193,129},{66,2},{130,66... | collective-permute-start | bytes 49160 | tf_op jit(solution)/shard_map/ppermute | solution.py:21
  156.2 3.3 %collective-permute-start.21 = (f32[2,16,128]{2,1,0:T(8,128)}, f32[2,16,128]{2,1,0:T(8,128)S(1)}, u32[]{:S(2)}, u32[]{:S(2)}) collective-permute-start(f32[2,16,128]{2,1,0:T(8,128)} %fusion.63), channel_id=1, source_target_pairs={{0,2},{2,4},{4,6},{6,8},{8,10},{10,12},{12,14},{14,16},{16,18},{18... | collective-permute-start | bytes 49160 | tf_op jit(solution)/shard_map/ppermute | solution.py:21
  159.7 2.4 %collective-permute-start.22 = (f32[2,256]{1,0:T(2,128)S(1)}, f32[2,256]{1,0:T(2,128)}, u32[]{:S(2)}, u32[]{:S(2)}) collective-permute-start(f32[2,256]{1,0:T(2,128)S(1)} %reshape_squeeze.31), channel_id=1, source_target_pairs={{0,1},{2,3},{4,5},{6,7},{8,9},{10,11},{12,13},{14,15},{16,17},{18,... | collective-permute-start | bytes 6152 | tf_op jit(solution)/shard_map/ppermute | solution.py:21
  162.8 2.8 %collective-permute-start.23 = (f32[2,16,128]{2,1,0:T(8,128)}, f32[2,16,128]{2,1,0:T(8,128)S(1)}, u32[]{:S(2)}, u32[]{:S(2)}) collective-permute-start(f32[2,16,128]{2,1,0:T(8,128)} %bitcast.40), channel_id=1, source_target_pairs={{0,64},{64,128},{128,192},{1,65},{65,129},{129,193},{2,66},{66,130... | collective-permute-start | bytes 49160 | tf_op jit(solution)/shard_map/ppermute | solution.py:21
  168.9 1.9 %fusion.6 = (f32[3,16,16,128]{3,2,1,0:T(8,128)}, f32[3,16,16,128]{3,2,1,0:T(8,128)S(1)}) fusion(f32[1,16,16,128]{3,2,1,0:T(8,128)S(1)} %get-tuple-element.64, f32[1,16,16,128]{3,2,1,0:T(8,128)S(1)} %get-tuple-element.65, f32[1,16,16,128]{3,2,1,0:T(8,128)S(1)} %get-tuple-element.63, f32[16,16,128]{2,1,0:T(8,128)} %get-tuple-element.30, ...), kind=kLoop, calls=%fused_computation.26 | loop fusion | flops 1867776 | bytes 3145728 | tf_op jit(solution)/shard_map/sub | solution.py:112
  172.2 1.9 %reduce.24 = f32[128,256]{1,0:T(8,128)S(1)} reduce(f32[128,1,256]{2,1,0:T(1,128)} %all-to-all-done, f32[]{:T(128)} %broadcast.190), dimensions={1}, to_apply=%all_to_all.12.reduce_sub_computation | reduce | bytes 262148 | tf_op jit(solution)/shard_map/all_to_all | solution.py:149
  174.2 1.8 fusion.24
  (196 shorter events, 80.5 us)
Async XLA Ops:
  1.7 40.9 %collective-permute-start = (f32[2,16,128]{2,1,0:T(8,128)S(1)}, f32[2,16,128]{2,1,0:T(8,128)S(1)}, u32[]{:S(2)}, u32[]{:S(2)}) collective-permute-start(f32[2,16,128]{2,1,0:T(8,128)S(1)} %fusion.57), channel_id=1, source_target_pairs={{2,0},{4,2},{6,4},{8,6},{10,8},{12,10},{14,12},{16,14},{18,16},{20... | collective-permute-start | bytes 49160 | tf_op jit(solution)/shard_map/ppermute | solution.py:21
  4.2 34.6 %collective-permute-start.1 = (f32[2,256]{1,0:T(2,128)S(1)}, f32[2,256]{1,0:T(2,128)S(1)}, u32[]{:S(2)}, u32[]{:S(2)}) collective-permute-start(f32[2,256]{1,0:T(2,128)S(1)} %reshape_squeeze.24), channel_id=1, source_target_pairs={{1,0},{3,2},{5,4},{7,6},{9,8},{11,10},{13,12},{15,14},{17,16},{19,... | collective-permute-start | bytes 6152 | tf_op jit(solution)/shard_map/ppermute | solution.py:21
  6.5 36.1 %collective-permute-start.2 = (f32[2,16,128]{2,1,0:T(8,128)S(1)}, f32[2,16,128]{2,1,0:T(8,128)S(1)}, u32[]{:S(2)}, u32[]{:S(2)}) collective-permute-start(f32[2,16,128]{2,1,0:T(8,128)S(1)} %bitcast.135), channel_id=1, source_target_pairs={{64,0},{128,64},{192,128},{65,1},{129,65},{193,129},{66,2},{130,66... | collective-permute-start | bytes 49160 | tf_op jit(solution)/shard_map/ppermute | solution.py:21
  13.4 27.2 %all-to-all-start.1 = ((f32[1,128,4]{2,0,1:T(1,128)}), f32[1,128,4]{2,0,1:T(1,128)S(1)}, u32[]{:S(2)}, u32[]{:S(2)}) async-start(f32[1,128,4]{2,0,1:T(1,128)} %bitcast.57), calls=%async_computation.1 | async-start | bytes 131072 | tf_op jit(solution)/shard_map/all_to_all | solution.py:150
  47.1 9.3 %collective-permute-start.3 = (f32[2,16,128]{2,1,0:T(8,128)}, f32[2,16,128]{2,1,0:T(8,128)S(1)}, u32[]{:S(2)}, u32[]{:S(2)}) collective-permute-start(f32[2,16,128]{2,1,0:T(8,128)} %fusion.58), channel_id=1, source_target_pairs={{0,2},{2,4},{4,6},{6,8},{8,10},{10,12},{12,14},{14,16},{16,18},{18... | collective-permute-start | bytes 49160 | tf_op jit(solution)/shard_map/ppermute | solution.py:21
  60.6 17.1 %collective-permute-start.6 = (f32[2,16,128]{2,1,0:T(8,128)S(1)}, f32[2,16,128]{2,1,0:T(8,128)S(1)}, u32[]{:S(2)}, u32[]{:S(2)}) collective-permute-start(f32[2,16,128]{2,1,0:T(8,128)S(1)} %fusion.59), channel_id=1, source_target_pairs={{2,0},{4,2},{6,4},{8,6},{10,8},{12,10},{14,12},{16,14},{18,16},{20... | collective-permute-start | bytes 49160 | tf_op jit(solution)/shard_map/ppermute | solution.py:21
  62.0 12.0 %collective-permute-start.7 = (f32[2,256]{1,0:T(2,128)S(1)}, f32[2,256]{1,0:T(2,128)S(1)}, u32[]{:S(2)}, u32[]{:S(2)}) collective-permute-start(f32[2,256]{1,0:T(2,128)S(1)} %reshape_squeeze.26), channel_id=1, source_target_pairs={{1,0},{3,2},{5,4},{7,6},{9,8},{11,10},{13,12},{15,14},{17,16},{19,... | collective-permute-start | bytes 6152 | tf_op jit(solution)/shard_map/ppermute | solution.py:21
  63.3 13.5 %collective-permute-start.13 = (f32[2,256]{1,0:T(2,128)S(1)}, f32[2,256]{1,0:T(2,128)S(1)}, u32[]{:S(2)}, u32[]{:S(2)}) collective-permute-start(f32[2,256]{1,0:T(2,128)S(1)} %reshape_squeeze.28), channel_id=1, source_target_pairs={{1,0},{3,2},{5,4},{7,6},{9,8},{11,10},{13,12},{15,14},{17,16},{19,... | collective-permute-start | bytes 6152 | tf_op jit(solution)/shard_map/ppermute | solution.py:21
  69.7 9.0 %collective-permute-start.8 = (f32[2,16,128]{2,1,0:T(8,128)S(1)}, f32[2,16,128]{2,1,0:T(8,128)S(1)}, u32[]{:S(2)}, u32[]{:S(2)}) collective-permute-start(f32[2,16,128]{2,1,0:T(8,128)S(1)} %bitcast.136), channel_id=1, source_target_pairs={{64,0},{128,64},{192,128},{65,1},{129,65},{193,129},{66,2},{130,66... | collective-permute-start | bytes 49160 | tf_op jit(solution)/shard_map/ppermute | solution.py:21
  72.7 9.5 %collective-permute-start.12 = (f32[2,16,128]{2,1,0:T(8,128)}, f32[2,16,128]{2,1,0:T(8,128)}, u32[]{:S(2)}, u32[]{:S(2)}) collective-permute-start(f32[2,16,128]{2,1,0:T(8,128)} %fusion.61), channel_id=1, source_target_pairs={{2,0},{4,2},{6,4},{8,6},{10,8},{12,10},{14,12},{16,14},{18,16},{20... | collective-permute-start | bytes 49160 | tf_op jit(solution)/shard_map/ppermute | solution.py:21
  74.0 9.2 %collective-permute-start.14 = (f32[2,16,128]{2,1,0:T(8,128)}, f32[2,16,128]{2,1,0:T(8,128)S(1)}, u32[]{:S(2)}, u32[]{:S(2)}) collective-permute-start(f32[2,16,128]{2,1,0:T(8,128)} %bitcast.25), channel_id=1, source_target_pairs={{64,0},{128,64},{192,128},{65,1},{129,65},{193,129},{66,2},{130,66... | collective-permute-start | bytes 49160 | tf_op jit(solution)/shard_map/ppermute | solution.py:21
  86.2 21.6 %collective-permute-start.9 = (f32[2,16,128]{2,1,0:T(8,128)S(1)}, f32[2,16,128]{2,1,0:T(8,128)S(1)}, u32[]{:S(2)}, u32[]{:S(2)}) collective-permute-start(f32[2,16,128]{2,1,0:T(8,128)S(1)} %fusion.60), channel_id=1, source_target_pairs={{0,2},{2,4},{4,6},{6,8},{8,10},{10,12},{12,14},{14,16},{16,18},{18... | collective-permute-start | bytes 49160 | tf_op jit(solution)/shard_map/ppermute | solution.py:21
  91.5 10.9 %collective-permute-start.10 = (f32[2,256]{1,0:T(2,128)S(1)}, f32[2,256]{1,0:T(2,128)S(1)}, u32[]{:S(2)}, u32[]{:S(2)}) collective-permute-start(f32[2,256]{1,0:T(2,128)S(1)} %reshape_squeeze.27), channel_id=1, source_target_pairs={{0,1},{2,3},{4,5},{6,7},{8,9},{10,11},{12,13},{14,15},{16,17},{18,... | collective-permute-start | bytes 6152 | tf_op jit(solution)/shard_map/ppermute | solution.py:21
  94.0 12.9 %collective-permute-start.16 = (f32[2,256]{1,0:T(2,128)S(1)}, f32[2,256]{1,0:T(2,128)S(1)}, u32[]{:S(2)}, u32[]{:S(2)}) collective-permute-start(f32[2,256]{1,0:T(2,128)S(1)} %reshape_squeeze.29), channel_id=1, source_target_pairs={{0,1},{2,3},{4,5},{6,7},{8,9},{10,11},{12,13},{14,15},{16,17},{18,... | collective-permute-start | bytes 6152 | tf_op jit(solution)/shard_map/ppermute | solution.py:21
  96.8 12.0 %collective-permute-start.11 = (f32[2,16,128]{2,1,0:T(8,128)S(1)}, f32[2,16,128]{2,1,0:T(8,128)S(1)}, u32[]{:S(2)}, u32[]{:S(2)}) collective-permute-start(f32[2,16,128]{2,1,0:T(8,128)S(1)} %bitcast.137), channel_id=1, source_target_pairs={{0,64},{64,128},{128,192},{1,65},{65,129},{129,193},{2,66},{66,130... | collective-permute-start | bytes 49160 | tf_op jit(solution)/shard_map/ppermute | solution.py:21
  100.4 9.7 %collective-permute-start.17 = (f32[2,16,128]{2,1,0:T(8,128)S(1)}, f32[2,16,128]{2,1,0:T(8,128)S(1)}, u32[]{:S(2)}, u32[]{:S(2)}) collective-permute-start(f32[2,16,128]{2,1,0:T(8,128)S(1)} %bitcast.129), channel_id=1, source_target_pairs={{0,64},{64,128},{128,192},{1,65},{65,129},{129,193},{2,66},{66,130... | collective-permute-start | bytes 49160 | tf_op jit(solution)/shard_map/ppermute | solution.py:21
  102.4 7.8 %collective-permute-start.15 = (f32[2,16,128]{2,1,0:T(8,128)S(1)}, f32[2,16,128]{2,1,0:T(8,128)S(1)}, u32[]{:S(2)}, u32[]{:S(2)}) collective-permute-start(f32[2,16,128]{2,1,0:T(8,128)S(1)} %fusion.56), channel_id=1, source_target_pairs={{0,2},{2,4},{4,6},{6,8},{8,10},{10,12},{12,14},{14,16},{16,18},{18... | collective-permute-start | bytes 49160 | tf_op jit(solution)/shard_map/ppermute | solution.py:21
  114.7 36.4 %collective-permute-start.18 = (f32[2,16,128]{2,1,0:T(8,128)}, f32[2,16,128]{2,1,0:T(8,128)S(1)}, u32[]{:S(2)}, u32[]{:S(2)}) collective-permute-start(f32[2,16,128]{2,1,0:T(8,128)} %fusion.62), channel_id=1, source_target_pairs={{2,0},{4,2},{6,4},{8,6},{10,8},{12,10},{14,12},{16,14},{18,16},{20... | collective-permute-start | bytes 49160 | tf_op jit(solution)/shard_map/ppermute | solution.py:21
  116.7 32.9 %collective-permute-start.19 = (f32[2,256]{1,0:T(2,128)}, f32[2,256]{1,0:T(2,128)}, u32[]{:S(2)}, u32[]{:S(2)}) collective-permute-start(f32[2,256]{1,0:T(2,128)} %reshape_squeeze.30), channel_id=1, source_target_pairs={{1,0},{3,2},{5,4},{7,6},{9,8},{11,10},{13,12},{15,14},{17,16},{19,... | collective-permute-start | bytes 6152 | tf_op jit(solution)/shard_map/ppermute | solution.py:21
  130.3 41.4 %all-to-all-start = ((f32[128,1,256]{2,1,0:T(1,128)}), f32[128,1,256]{2,1,0:T(1,128)}, u32[]{:S(2)}, u32[]{:S(2)}) async-start(f32[128,1,256]{2,1,0:T(1,128)} %reshape.198), calls=%async_computation | async-start | bytes 262144 | tf_op jit(solution)/shard_map/all_to_all | solution.py:149
  147.3 6.2 %collective-permute-start.20 = (f32[2,16,128]{2,1,0:T(8,128)}, f32[2,16,128]{2,1,0:T(8,128)S(1)}, u32[]{:S(2)}, u32[]{:S(2)}) collective-permute-start(f32[2,16,128]{2,1,0:T(8,128)} %bitcast.138), channel_id=1, source_target_pairs={{64,0},{128,64},{192,128},{65,1},{129,65},{193,129},{66,2},{130,66... | collective-permute-start | bytes 49160 | tf_op jit(solution)/shard_map/ppermute | solution.py:21
  156.2 10.2 %collective-permute-start.21 = (f32[2,16,128]{2,1,0:T(8,128)}, f32[2,16,128]{2,1,0:T(8,128)S(1)}, u32[]{:S(2)}, u32[]{:S(2)}) collective-permute-start(f32[2,16,128]{2,1,0:T(8,128)} %fusion.63), channel_id=1, source_target_pairs={{0,2},{2,4},{4,6},{6,8},{8,10},{10,12},{12,14},{14,16},{16,18},{18... | collective-permute-start | bytes 49160 | tf_op jit(solution)/shard_map/ppermute | solution.py:21
  159.7 5.9 %collective-permute-start.22 = (f32[2,256]{1,0:T(2,128)S(1)}, f32[2,256]{1,0:T(2,128)}, u32[]{:S(2)}, u32[]{:S(2)}) collective-permute-start(f32[2,256]{1,0:T(2,128)S(1)} %reshape_squeeze.31), channel_id=1, source_target_pairs={{0,1},{2,3},{4,5},{6,7},{8,9},{10,11},{12,13},{14,15},{16,17},{18,... | collective-permute-start | bytes 6152 | tf_op jit(solution)/shard_map/ppermute | solution.py:21
  162.8 5.8 %collective-permute-start.23 = (f32[2,16,128]{2,1,0:T(8,128)}, f32[2,16,128]{2,1,0:T(8,128)S(1)}, u32[]{:S(2)}, u32[]{:S(2)}) collective-permute-start(f32[2,16,128]{2,1,0:T(8,128)} %bitcast.40), channel_id=1, source_target_pairs={{0,64},{64,128},{128,192},{1,65},{65,129},{129,193},{2,66},{66,130... | collective-permute-start | bytes 49160 | tf_op jit(solution)/shard_map/ppermute | solution.py:21
  (17 other events, 368.5 us)
where the time goes:
time: 178 us; the launch traced here: 176 us
  starting transfers between devices  88.3 us (50%)
  other arithmetic  41.9 us (24%)
  local copies, waits for them, and re-layouts  28.3 us (16%)
  matrix products  10 us (6%)
  waiting for transfers between devices  5.8 us (3%)
    ppermute x24, starting transfers between devices, passed_along(): return lax.ppermute(x, axis, pairs)  54.4 us
    all_to_all x1, starting transfers between devices, local(): lax.all_to_all(send_vals, ('bx', 'by'), split_axis=1, concat_axis=1, tile...  17 us
    all_to_all x1, starting transfers between devices, local(): lax.all_to_all(send_ids, ('bx', 'by'), split_axis=1, concat_axis=1, tiled...  16.9 us
    sub x8, other arithmetic, differ(): return neighbour - couple  7.75 us
    another operation x8, local copies, waits for them, and re-layouts, beside(): arrived = jnp.expand_dims(arrived, axis_dim)  7.18 us
    dot_general x1, matrix products, local(): jnp.einsum('tfkc,tc->tfk', blocks, cell_tiles, preferred_element_type=jnp...  6.71 us
    slice x8, local copies, waits for them, and re-layouts, beside(): lax.slice_in_dim(couple, 1, length, axis=axis_dim)  5.3 us
    slice x13, local copies, waits for them, and re-layouts, beside(): lax.index_in_dim(couple, border_at, axis=axis_dim, keepdims=False)  5.01 us
  transfers between devices with their start and end apart: 26, of which 4 were waited for; matrix products, arithmetic and copies ran while one was open for 34% of the time, Pallas kernels for 0%

commit v1 on v0

--- a/solution.py
+++ b/solution.py
@@ -146,7 +146,15 @@
         - 1.0
     )
     got_vals, got_ids = (
-        lax.all_to_all(send_vals, ("bx", "by"), split_axis=1, concat_axis=1, tiled=True),
+        jnp.concatenate(
+            lax.all_to_all(
+                jnp.stack(jnp.split(send_vals, lax.axis_size(("bx", "by")), axis=1)),
+                ("bx", "by"),
+                0,
+                0,
+            ),
+            axis=1,
+        ),
         lax.all_to_all(send_ids, ("bx", "by"), split_axis=1, concat_axis=1, tiled=True),
     )
     group_hits = (

time: 178 us -> 269 us (1.51)
  local copies, waits for them, and re-layouts: 28.3 us -> 120 us
    unnamed x33 -> x172, local copies, waits for them, and re-layouts: 2.72 us -> 88.8 us
    ppermute x24, starting transfers between devices: 54.4 us -> 59.4 us  [passed_along(): return lax.ppermute(x, axis, pairs)]
    another operation x4 -> x6, local copies, waits for them, and re-layouts: 0.02 us -> 4.31 us  [the longest x2 4.29 us: local(): jnp.stack(jnp.split(send_vals, lax.axis_size(('bx', 'by')), axis=1))]
    all_to_all x1, starting transfers between devices: 17 us -> 14.2 us  [local(): lax.all_to_all(jnp.stack(jnp.split(send_vals, lax.axis_size(('bx', 'by'))...]
  transfers between devices with their start and end apart: 26 -> 26, of which waited for: 4 -> 3; matrix products, arithmetic and copies ran while one was open for 34% -> 57% of each run, Pallas kernels for 0% -> 0%
where the time goes in v1:
time: 269 us; the launch traced here: 267 us
  local copies, waits for them, and re-layouts  120 us (45%)
  starting transfers between devices  90.6 us (34%)
  other arithmetic  39.5 us (15%)
  matrix products  9.19 us (3%)
  waiting for transfers between devices  5.85 us (2%)
    unnamed x172, local copies, waits for them, and re-layouts  88.8 us
    ppermute x24, starting transfers between devices, passed_along(): return lax.ppermute(x, axis, pairs)  59.4 us
    all_to_all x1, starting transfers between devices, local(): lax.all_to_all(send_ids, ('bx', 'by'), split_axis=1, concat_axis=1, tiled...  16.9 us
    all_to_all x1, starting transfers between devices, local(): lax.all_to_all(jnp.stack(jnp.split(send_vals, lax.axis_size(('bx', 'by'))...  14.2 us
    another operation x8, local copies, waits for them, and re-layouts, beside(): arrived = jnp.expand_dims(arrived, axis_dim)  7.73 us
    dot_general x1, matrix products, local(): jnp.einsum('tfkc,tc->tfk', blocks, cell_tiles, preferred_element_type=jnp...  6.71 us
    slice x13, local copies, waits for them, and re-layouts, beside(): lax.index_in_dim(couple, border_at, axis=axis_dim, keepdims=False)  6.27 us
    sub x8, other arithmetic, differ(): return neighbour - couple  6.24 us
  transfers between devices with their start and end apart: 26, of which 3 were waited for; matrix products, arithmetic and copies ran while one was open for 57% of the time, Pallas kernels for 0%

profile of v1, /device:TPU:4, one launch (start us, length us, event | category | flops | bytes accessed | tf_op | source)
XLA Modules:
  0.0 267.3 jit_solution(5432639141790778856)
XLA Ops:
  4.1 2.4 collective-permute-start.2
  13.3 16.9 %all-to-all-start.1 = ((f32[1,128,4]{2,0,1:T(1,128)}), f32[1,128,4]{2,0,1:T(1,128)S(1)}, u32[]{:S(2)}, u32[]{:S(2)}) async-start(f32[1,128,4]{2,0,1:T(1,128)} %bitcast.185), calls=%async_computation.1 | async-start | bytes 131072 | tf_op jit(solution)/shard_map/all_to_all | solution.py:158
  36.6 3.8 %all-to-all-done.1 = f32[1,128,4]{2,0,1:T(1,128)S(1)} async-done(((f32[1,128,4]{2,0,1:T(1,128)}), f32[1,128,4]{2,0,1:T(1,128)S(1)}, u32[]{:S(2)}, u32[]{:S(2)}) %all-to-all-start.1) | async-done | bytes 2080 | tf_op jit(solution)/shard_map/all_to_all | solution.py:158
  43.6 1.8 collective-permute-start.4
  46.1 3.1 %collective-permute-start.3 = (f32[2,16,128]{2,1,0:T(8,128)}, f32[2,16,128]{2,1,0:T(8,128)}, u32[]{:S(2)}, u32[]{:S(2)}) collective-permute-start(f32[2,16,128]{2,1,0:T(8,128)} %fusion.56), channel_id=1, source_target_pairs={{0,2},{2,4},{4,6},{6,8},{8,10},{10,12},{12,14},{14,16},{16,18},{18... | collective-permute-start | bytes 49160 | tf_op jit(solution)/shard_map/ppermute | solution.py:21
  50.5 2.6 collective-permute-start.5
  70.9 3.0 %collective-permute-start.14 = (f32[2,16,128]{2,1,0:T(8,128)}, f32[2,16,128]{2,1,0:T(8,128)S(1)}, u32[]{:S(2)}, u32[]{:S(2)}) collective-permute-start(f32[2,16,128]{2,1,0:T(8,128)} %bitcast.25), channel_id=1, source_target_pairs={{64,0},{128,64},{192,128},{65,1},{129,65},{193,129},{66,2},{130,66... | collective-permute-start | bytes 49160 | tf_op jit(solution)/shard_map/ppermute | solution.py:21
  73.9 1.9 collective-permute-start.8
  88.6 3.8 %collective-permute-start.16 = (f32[2,256]{1,0:T(2,128)S(1)}, f32[2,256]{1,0:T(2,128)S(1)}, u32[]{:S(2)}, u32[]{:S(2)}) collective-permute-start(f32[2,256]{1,0:T(2,128)S(1)} %reshape_squeeze.29), channel_id=1, source_target_pairs={{0,1},{2,3},{4,5},{6,7},{8,9},{10,11},{12,13},{14,15},{16,17},{18,... | collective-permute-start | bytes 6152 | tf_op jit(solution)/shard_map/ppermute | solution.py:21
  92.5 4.9 %collective-permute-start.15 = (f32[2,16,128]{2,1,0:T(8,128)}, f32[2,16,128]{2,1,0:T(8,128)S(1)}, u32[]{:S(2)}, u32[]{:S(2)}) collective-permute-start(f32[2,16,128]{2,1,0:T(8,128)} %fusion.54), channel_id=1, source_target_pairs={{0,2},{2,4},{4,6},{6,8},{8,10},{10,12},{12,14},{14,16},{16,18},{18... | collective-permute-start | bytes 49160 | tf_op jit(solution)/shard_map/ppermute | solution.py:21
  97.4 4.2 %collective-permute-start.17 = (f32[2,16,128]{2,1,0:T(8,128)}, f32[2,16,128]{2,1,0:T(8,128)S(1)}, u32[]{:S(2)}, u32[]{:S(2)}) collective-permute-start(f32[2,16,128]{2,1,0:T(8,128)} %bitcast.639), channel_id=1, source_target_pairs={{0,64},{64,128},{128,192},{1,65},{65,129},{129,193},{2,66},{66,130... | collective-permute-start | bytes 49160 | tf_op jit(solution)/shard_map/ppermute | solution.py:21
  105.1 1.9 collective-permute-start.11
  107.1 3.6 %collective-permute-start.9 = (f32[2,16,128]{2,1,0:T(8,128)S(1)}, f32[2,16,128]{2,1,0:T(8,128)S(1)}, u32[]{:S(2)}, u32[]{:S(2)}) collective-permute-start(f32[2,16,128]{2,1,0:T(8,128)S(1)} %fusion.58), channel_id=1, source_target_pairs={{0,2},{2,4},{4,6},{6,8},{8,10},{10,12},{12,14},{14,16},{16,18},{18... | collective-permute-start | bytes 49160 | tf_op jit(solution)/shard_map/ppermute | solution.py:21
  114.5 1.9 multiply_reduce_fusion.1
  120.7 3.9 %collective-permute-start.20 = (f32[2,16,128]{2,1,0:T(8,128)}, f32[2,16,128]{2,1,0:T(8,128)S(1)}, u32[]{:S(2)}, u32[]{:S(2)}) collective-permute-start(f32[2,16,128]{2,1,0:T(8,128)} %bitcast.35), channel_id=1, source_target_pairs={{64,0},{128,64},{192,128},{65,1},{129,65},{193,129},{66,2},{130,66... | collective-permute-start | bytes 49160 | tf_op jit(solution)/shard_map/ppermute | solution.py:21
  128.8 6.7 %fusion.68 = f32[128,1,2,64]{3,1,2,0:T(1,128)S(1)} fusion(bf16[128,256,1,1]{1,2,3,0:T(2,128)(2,1)S(1)} %reshape.165, bf16[128,2,64,256]{3,2,1,0:T(8,128)(2,1)} %bitcast.622), kind=kOutput, calls=%fused_computation.457 | convolution fusion | flops 8388608 | bytes 8519680 | tf_op jit(solution)/shard_map/tfkc,tc->tfk/dot_general | solution.py:123
  222.6 3.6 %copy.239 = f32[128,64,4]{1,2,0:T(4,128)} copy(f32[128,64,4]{2,1,0:T(8,128)} %constant_dynamic-update-slice_fusion) | data formatting | bytes 262144 | tf_op jit(solution)/shard_map/stack | solution.py:151
  226.2 1.8 reshape.185
  228.0 14.2 %all-to-all-start = ((f32[128,1,256]{2,1,0:T(1,128)}), f32[128,1,256]{2,1,0:T(1,128)}, u32[]{:S(2)}, u32[]{:S(2)}) async-start(f32[128,1,256]{2,1,0:T(1,128)} %reshape.185), calls=%async_computation | async-start | bytes 262144 | tf_op jit(solution)/shard_map/all_to_all | solution.py:150
  247.2 3.0 %collective-permute-start.22 = (f32[2,256]{1,0:T(2,128)S(1)}, f32[2,256]{1,0:T(2,128)}, u32[]{:S(2)}, u32[]{:S(2)}) collective-permute-start(f32[2,256]{1,0:T(2,128)S(1)} %reshape_squeeze.31), channel_id=1, source_target_pairs={{0,1},{2,3},{4,5},{6,7},{8,9},{10,11},{12,13},{14,15},{16,17},{18,... | collective-permute-start | bytes 6152 | tf_op jit(solution)/shard_map/ppermute | solution.py:21
  250.2 4.0 %collective-permute-start.21 = (f32[2,16,128]{2,1,0:T(8,128)S(1)}, f32[2,16,128]{2,1,0:T(8,128)}, u32[]{:S(2)}, u32[]{:S(2)}) collective-permute-start(f32[2,16,128]{2,1,0:T(8,128)S(1)} %fusion.61), channel_id=1, source_target_pairs={{0,2},{2,4},{4,6},{6,8},{8,10},{10,12},{12,14},{14,16},{16,18},{18... | collective-permute-start | bytes 49160 | tf_op jit(solution)/shard_map/ppermute | solution.py:21
  254.8 3.4 %collective-permute-start.23 = (f32[2,16,128]{2,1,0:T(8,128)}, f32[2,16,128]{2,1,0:T(8,128)S(1)}, u32[]{:S(2)}, u32[]{:S(2)}) collective-permute-start(f32[2,16,128]{2,1,0:T(8,128)} %bitcast.40), channel_id=1, source_target_pairs={{0,64},{64,128},{128,192},{1,65},{65,129},{129,193},{2,66},{66,130... | collective-permute-start | bytes 49160 | tf_op jit(solution)/shard_map/ppermute | solution.py:21
  261.0 1.9 fusion.5
  263.5 1.9 reduce.24
  (335 shorter events, 165.1 us)
Async XLA Ops:
  1.9 34.5 %collective-permute-start.1 = (f32[2,256]{1,0:T(2,128)S(1)}, f32[2,256]{1,0:T(2,128)S(1)}, u32[]{:S(2)}, u32[]{:S(2)}) collective-permute-start(f32[2,256]{1,0:T(2,128)S(1)} %reshape_squeeze.24), channel_id=1, source_target_pairs={{1,0},{3,2},{5,4},{7,6},{9,8},{11,10},{13,12},{15,14},{17,16},{19,... | collective-permute-start | bytes 6152 | tf_op jit(solution)/shard_map/ppermute | solution.py:21
  4.1 38.3 %collective-permute-start.2 = (f32[2,16,128]{2,1,0:T(8,128)S(1)}, f32[2,16,128]{2,1,0:T(8,128)S(1)}, u32[]{:S(2)}, u32[]{:S(2)}) collective-permute-start(f32[2,16,128]{2,1,0:T(8,128)S(1)} %bitcast.642), channel_id=1, source_target_pairs={{64,0},{128,64},{192,128},{65,1},{129,65},{193,129},{66,2},{130,66... | collective-permute-start | bytes 49160 | tf_op jit(solution)/shard_map/ppermute | solution.py:21
  7.5 34.8 %collective-permute-start = (f32[2,16,128]{2,1,0:T(8,128)S(1)}, f32[2,16,128]{2,1,0:T(8,128)S(1)}, u32[]{:S(2)}, u32[]{:S(2)}) collective-permute-start(f32[2,16,128]{2,1,0:T(8,128)S(1)} %fusion.55), channel_id=1, source_target_pairs={{2,0},{4,2},{6,4},{8,6},{10,8},{12,10},{14,12},{16,14},{18,16},{20... | collective-permute-start | bytes 49160 | tf_op jit(solution)/shard_map/ppermute | solution.py:21
  13.3 27.0 %all-to-all-start.1 = ((f32[1,128,4]{2,0,1:T(1,128)}), f32[1,128,4]{2,0,1:T(1,128)S(1)}, u32[]{:S(2)}, u32[]{:S(2)}) async-start(f32[1,128,4]{2,0,1:T(1,128)} %bitcast.185), calls=%async_computation.1 | async-start | bytes 131072 | tf_op jit(solution)/shard_map/all_to_all | solution.py:158
  43.6 9.5 %collective-permute-start.4 = (f32[2,256]{1,0:T(2,128)S(1)}, f32[2,256]{1,0:T(2,128)}, u32[]{:S(2)}, u32[]{:S(2)}) collective-permute-start(f32[2,256]{1,0:T(2,128)S(1)} %reshape_squeeze.25), channel_id=1, source_target_pairs={{0,1},{2,3},{4,5},{6,7},{8,9},{10,11},{12,13},{14,15},{16,17},{18,... | collective-permute-start | bytes 6152 | tf_op jit(solution)/shard_map/ppermute | solution.py:21
  46.1 7.9 %collective-permute-start.3 = (f32[2,16,128]{2,1,0:T(8,128)}, f32[2,16,128]{2,1,0:T(8,128)}, u32[]{:S(2)}, u32[]{:S(2)}) collective-permute-start(f32[2,16,128]{2,1,0:T(8,128)} %fusion.56), channel_id=1, source_target_pairs={{0,2},{2,4},{4,6},{6,8},{8,10},{10,12},{12,14},{14,16},{16,18},{18... | collective-permute-start | bytes 49160 | tf_op jit(solution)/shard_map/ppermute | solution.py:21
  60.0 15.9 %collective-permute-start.13 = (f32[2,256]{1,0:T(2,128)}, f32[2,256]{1,0:T(2,128)}, u32[]{:S(2)}, u32[]{:S(2)}) collective-permute-start(f32[2,256]{1,0:T(2,128)} %reshape_squeeze.28), channel_id=1, source_target_pairs={{1,0},{3,2},{5,4},{7,6},{9,8},{11,10},{13,12},{15,14},{17,16},{19,... | collective-permute-start | bytes 6152 | tf_op jit(solution)/shard_map/ppermute | solution.py:21
  61.3 19.0 %collective-permute-start.12 = (f32[2,16,128]{2,1,0:T(8,128)}, f32[2,16,128]{2,1,0:T(8,128)}, u32[]{:S(2)}, u32[]{:S(2)}) collective-permute-start(f32[2,16,128]{2,1,0:T(8,128)} %fusion.59), channel_id=1, source_target_pairs={{2,0},{4,2},{6,4},{8,6},{10,8},{12,10},{14,12},{16,14},{18,16},{20... | collective-permute-start | bytes 49160 | tf_op jit(solution)/shard_map/ppermute | solution.py:21
  64.0 14.8 %collective-permute-start.7 = (f32[2,256]{1,0:T(2,128)}, f32[2,256]{1,0:T(2,128)}, u32[]{:S(2)}, u32[]{:S(2)}) collective-permute-start(f32[2,256]{1,0:T(2,128)} %reshape_squeeze.26), channel_id=1, source_target_pairs={{1,0},{3,2},{5,4},{7,6},{9,8},{11,10},{13,12},{15,14},{17,16},{19,... | collective-permute-start | bytes 6152 | tf_op jit(solution)/shard_map/ppermute | solution.py:21
  70.9 10.5 %collective-permute-start.14 = (f32[2,16,128]{2,1,0:T(8,128)}, f32[2,16,128]{2,1,0:T(8,128)S(1)}, u32[]{:S(2)}, u32[]{:S(2)}) collective-permute-start(f32[2,16,128]{2,1,0:T(8,128)} %bitcast.25), channel_id=1, source_target_pairs={{64,0},{128,64},{192,128},{65,1},{129,65},{193,129},{66,2},{130,66... | collective-permute-start | bytes 49160 | tf_op jit(solution)/shard_map/ppermute | solution.py:21
  73.9 13.3 %collective-permute-start.8 = (f32[2,16,128]{2,1,0:T(8,128)}, f32[2,16,128]{2,1,0:T(8,128)}, u32[]{:S(2)}, u32[]{:S(2)}) collective-permute-start(f32[2,16,128]{2,1,0:T(8,128)} %bitcast.14), channel_id=1, source_target_pairs={{64,0},{128,64},{192,128},{65,1},{129,65},{193,129},{66,2},{130,66... | collective-permute-start | bytes 49160 | tf_op jit(solution)/shard_map/ppermute | solution.py:21
  75.9 9.7 %collective-permute-start.6 = (f32[2,16,128]{2,1,0:T(8,128)}, f32[2,16,128]{2,1,0:T(8,128)}, u32[]{:S(2)}, u32[]{:S(2)}) collective-permute-start(f32[2,16,128]{2,1,0:T(8,128)} %fusion.57), channel_id=1, source_target_pairs={{2,0},{4,2},{6,4},{8,6},{10,8},{12,10},{14,12},{16,14},{18,16},{20... | collective-permute-start | bytes 49160 | tf_op jit(solution)/shard_map/ppermute | solution.py:21
  88.6 18.4 %collective-permute-start.16 = (f32[2,256]{1,0:T(2,128)S(1)}, f32[2,256]{1,0:T(2,128)S(1)}, u32[]{:S(2)}, u32[]{:S(2)}) collective-permute-start(f32[2,256]{1,0:T(2,128)S(1)} %reshape_squeeze.29), channel_id=1, source_target_pairs={{0,1},{2,3},{4,5},{6,7},{8,9},{10,11},{12,13},{14,15},{16,17},{18,... | collective-permute-start | bytes 6152 | tf_op jit(solution)/shard_map/ppermute | solution.py:21
  92.5 19.4 %collective-permute-start.15 = (f32[2,16,128]{2,1,0:T(8,128)}, f32[2,16,128]{2,1,0:T(8,128)S(1)}, u32[]{:S(2)}, u32[]{:S(2)}) collective-permute-start(f32[2,16,128]{2,1,0:T(8,128)} %fusion.54), channel_id=1, source_target_pairs={{0,2},{2,4},{4,6},{6,8},{8,10},{10,12},{12,14},{14,16},{16,18},{18... | collective-permute-start | bytes 49160 | tf_op jit(solution)/shard_map/ppermute | solution.py:21
  97.4 14.5 %collective-permute-start.17 = (f32[2,16,128]{2,1,0:T(8,128)}, f32[2,16,128]{2,1,0:T(8,128)S(1)}, u32[]{:S(2)}, u32[]{:S(2)}) collective-permute-start(f32[2,16,128]{2,1,0:T(8,128)} %bitcast.639), channel_id=1, source_target_pairs={{0,64},{64,128},{128,192},{1,65},{65,129},{129,193},{2,66},{66,130... | collective-permute-start | bytes 49160 | tf_op jit(solution)/shard_map/ppermute | solution.py:21
  101.7 9.3 %collective-permute-start.10 = (f32[2,256]{1,0:T(2,128)S(1)}, f32[2,256]{1,0:T(2,128)S(1)}, u32[]{:S(2)}, u32[]{:S(2)}) collective-permute-start(f32[2,256]{1,0:T(2,128)S(1)} %reshape_squeeze.27), channel_id=1, source_target_pairs={{0,1},{2,3},{4,5},{6,7},{8,9},{10,11},{12,13},{14,15},{16,17},{18,... | collective-permute-start | bytes 6152 | tf_op jit(solution)/shard_map/ppermute | solution.py:21
  105.1 9.2 %collective-permute-start.11 = (f32[2,16,128]{2,1,0:T(8,128)S(1)}, f32[2,16,128]{2,1,0:T(8,128)S(1)}, u32[]{:S(2)}, u32[]{:S(2)}) collective-permute-start(f32[2,16,128]{2,1,0:T(8,128)S(1)} %bitcast.643), channel_id=1, source_target_pairs={{0,64},{64,128},{128,192},{1,65},{65,129},{129,193},{2,66},{66,130... | collective-permute-start | bytes 49160 | tf_op jit(solution)/shard_map/ppermute | solution.py:21
  107.1 6.2 %collective-permute-start.9 = (f32[2,16,128]{2,1,0:T(8,128)S(1)}, f32[2,16,128]{2,1,0:T(8,128)S(1)}, u32[]{:S(2)}, u32[]{:S(2)}) collective-permute-start(f32[2,16,128]{2,1,0:T(8,128)S(1)} %fusion.58), channel_id=1, source_target_pairs={{0,2},{2,4},{4,6},{6,8},{8,10},{10,12},{12,14},{14,16},{16,18},{18... | collective-permute-start | bytes 49160 | tf_op jit(solution)/shard_map/ppermute | solution.py:21
  119.4 122.8 %collective-permute-start.19 = (f32[2,256]{1,0:T(2,128)}, f32[2,256]{1,0:T(2,128)}, u32[]{:S(2)}, u32[]{:S(2)}) collective-permute-start(f32[2,256]{1,0:T(2,128)} %reshape_squeeze.30), channel_id=1, source_target_pairs={{1,0},{3,2},{5,4},{7,6},{9,8},{11,10},{13,12},{15,14},{17,16},{19,... | collective-permute-start | bytes 6152 | tf_op jit(solution)/shard_map/ppermute | solution.py:21
  120.7 124.1 %collective-permute-start.20 = (f32[2,16,128]{2,1,0:T(8,128)}, f32[2,16,128]{2,1,0:T(8,128)S(1)}, u32[]{:S(2)}, u32[]{:S(2)}) collective-permute-start(f32[2,16,128]{2,1,0:T(8,128)} %bitcast.35), channel_id=1, source_target_pairs={{64,0},{128,64},{192,128},{65,1},{129,65},{193,129},{66,2},{130,66... | collective-permute-start | bytes 49160 | tf_op jit(solution)/shard_map/ppermute | solution.py:21
  124.6 119.2 %collective-permute-start.18 = (f32[2,16,128]{2,1,0:T(8,128)}, f32[2,16,128]{2,1,0:T(8,128)}, u32[]{:S(2)}, u32[]{:S(2)}) collective-permute-start(f32[2,16,128]{2,1,0:T(8,128)} %fusion.60), channel_id=1, source_target_pairs={{2,0},{4,2},{6,4},{8,6},{10,8},{12,10},{14,12},{16,14},{18,16},{20... | collective-permute-start | bytes 49160 | tf_op jit(solution)/shard_map/ppermute | solution.py:21
  228.0 34.9 %all-to-all-start = ((f32[128,1,256]{2,1,0:T(1,128)}), f32[128,1,256]{2,1,0:T(1,128)}, u32[]{:S(2)}, u32[]{:S(2)}) async-start(f32[128,1,256]{2,1,0:T(1,128)} %reshape.185), calls=%async_computation | async-start | bytes 262144 | tf_op jit(solution)/shard_map/all_to_all | solution.py:150
  247.2 11.1 %collective-permute-start.22 = (f32[2,256]{1,0:T(2,128)S(1)}, f32[2,256]{1,0:T(2,128)}, u32[]{:S(2)}, u32[]{:S(2)}) collective-permute-start(f32[2,256]{1,0:T(2,128)S(1)} %reshape_squeeze.31), channel_id=1, source_target_pairs={{0,1},{2,3},{4,5},{6,7},{8,9},{10,11},{12,13},{14,15},{16,17},{18,... | collective-permute-start | bytes 6152 | tf_op jit(solution)/shard_map/ppermute | solution.py:21
  250.2 8.9 %collective-permute-start.21 = (f32[2,16,128]{2,1,0:T(8,128)S(1)}, f32[2,16,128]{2,1,0:T(8,128)}, u32[]{:S(2)}, u32[]{:S(2)}) collective-permute-start(f32[2,16,128]{2,1,0:T(8,128)S(1)} %fusion.61), channel_id=1, source_target_pairs={{0,2},{2,4},{4,6},{6,8},{8,10},{10,12},{12,14},{14,16},{16,18},{18... | collective-permute-start | bytes 49160 | tf_op jit(solution)/shard_map/ppermute | solution.py:21
  (23 other events, 179.2 us)
